TPU v7x, 256 devices: a whole 4x4x8 slice. The times are simulated.
256 devices in a mesh: dp: 32 (over y, x, core), tsp: 8 (over z).
Axes of the slice: x: 4, y: 4, z: 8, core: 2. Of those that a mesh axis runs over, the one named last changes fastest.
Arguments:
- tokens: bfloat16 [65536, 8192], P('dp', 'tsp'), may hold values from -6 to 6
- cotangent: bfloat16 [65536, 1024], P('dp', 'tsp'), may hold values from -6 to 6
- frozen_key_weight: bfloat16 [8192, 1024], P('tsp'), may hold values from -0.1875 to 0.1875
- adapter_down_weight: bfloat16 [64, 64, 8192], P('dp', None, 'tsp'), may hold values from -0.0625 to 0.0625
- adapter_up_weight: bfloat16 [64, 64, 1024], P('dp', None, 'tsp'), may hold values from -0.1875 to 0.1875
- adapter_place_table: int32 [64], replicated, may hold values from 0 to 63, as said below
- segment_adapter: int32 [512], P('dp'), may hold values from 0 to 63, as said below
- segment_live_count: int32 [512], P('dp'), may hold values from 1 to 128, as said below
Outputs:
- token_gradient: bfloat16 [65536, 8192], P('dp', 'tsp')
- down_grad: float32 [64, 64, 8192], P('dp', None, 'tsp')
- up_grad: float32 [64, 64, 1024], P('dp', None, 'tsp')
Inputs may be any that keep to these rules, and one draw needn't show every extreme that they name: A permutation: adapter a is held at place adapter_place_table[a], that is by the dp index adapter_place_table[a] // 2 as its entry adapter_place_table[a] % 2; the adapters' arrays and gradients are indexed by place. `segment_adapter`: the 16 segments of one dp index name at most one adapter held by any one dp index; an adapter may be named by several of them. `segment_live_count`: the live rows stand at the start of each segment; on every dp index some segment is full.
All inputs are finite; a program needn't handle non-finite values.
Results may differ from a plain program's by a relative error of at most 0.0034.
Values may be sent and summed in bfloat16 or wider, within the bound.
A program may use at most 128 MiB of HBM per device.

v0:
```python
import jax
import jax.numpy as jnp
from jax import lax
from jax.sharding import PartitionSpec as P

ADAPTER_SCALE = 2.0


def lookup(idents, mapping):
    matches = idents[:, None] == jnp.arange(mapping.shape[0], dtype=jnp.int32)[None, :]
    return jnp.sum(jnp.where(matches, mapping[None, :], 0), axis=1)


def on_device(
    tokens,
    cotangent,
    frozen_key_weight,
    adapter_down_weight,
    adapter_up_weight,
    adapter_place_table,
    segment_adapter,
    segment_live_count,
):
    dp_count = lax.axis_size("dp")
    places_per_device = adapter_down_weight.shape[0]
    rank_of_adapter = adapter_down_weight.shape[1]
    width_per_device = tokens.shape[1]
    key_dev = cotangent.shape[1]
    segments_per_device = segment_adapter.shape[0]
    segment_token_rows = tokens.shape[0] // segments_per_device
    adapter_places = lookup(segment_adapter, adapter_place_table)
    seg_owner = adapter_places // places_per_device
    seg_entry = adapter_places % places_per_device
    owner_hit = seg_owner[:, None] == jnp.arange(dp_count, dtype=jnp.int32)[None, :]
    wanted = jnp.max(jnp.where(owner_hit, seg_entry[:, None], -1), axis=0)
    incoming = lax.all_to_all(wanted[:, None], "dp", split_axis=0, concat_axis=0, tiled=True)[:, 0]
    serving_mesh = (
        incoming[:, None] == jnp.arange(places_per_device, dtype=jnp.int32)[None, :]
    ).astype(jnp.bfloat16)
    reply_down = jnp.einsum(
        "ap,phc->ahc", serving_mesh, adapter_down_weight, preferred_element_type=jnp.float32
    ).astype(jnp.bfloat16)
    reply_up = jnp.einsum(
        "hv,vun->hun", serving_mesh, adapter_up_weight, preferred_element_type=jnp.float32
    ).astype(jnp.bfloat16)
    fetched_down, fetched_up = (
        lax.all_to_all(reply_down, "dp", split_axis=0, concat_axis=0, tiled=True),
        lax.all_to_all(reply_up, "dp", split_axis=0, concat_axis=0, tiled=True),
    )
    picker = owner_hit.astype(jnp.bfloat16)
    segment_down_weight = jnp.einsum(
        "go,ord->grd", picker, fetched_down, preferred_element_type=jnp.float32
    ).astype(jnp.bfloat16)
    segment_up_weight = jnp.einsum(
        "go,ork->grk", picker, fetched_up, preferred_element_type=jnp.float32
    ).astype(jnp.bfloat16)
    seg_tokens = tokens.reshape(segments_per_device, segment_token_rows, width_per_device)
    seg_cotangent = cotangent.reshape(segments_per_device, segment_token_rows, key_dev)
    live_rows = (
        jnp.arange(segment_token_rows, dtype=jnp.int32)[None, :] < segment_live_count[:, None]
    ).astype(jnp.float32)
    partial_terms = jnp.concatenate(
        [
            jnp.einsum(
                "gtd,grd->gtr", seg_tokens, segment_down_weight, preferred_element_type=jnp.float32
            ),
            jnp.einsum(
                "gtk,grk->gtr", seg_cotangent, segment_up_weight, preferred_element_type=jnp.float32
            ),
        ],
        axis=2,
    )
    summed = lax.psum(partial_terms, "tsp")
    reduced_rows = (summed[:, :, :rank_of_adapter] * live_rows[:, :, None]).astype(jnp.bfloat16)
    gathered_weights = (summed[:, :, rank_of_adapter:] * live_rows[:, :, None]).astype(jnp.bfloat16)
    frozen_output = lax.dot_general(
        lax.all_gather(cotangent, "tsp", axis=1, tiled=True),
        frozen_key_weight,
        (((1,), (1,)), ((), ())),
        preferred_element_type=jnp.float32,
    )
    adapter_output = jnp.einsum(
        "wks,wsx->wkx", gathered_weights, segment_down_weight, preferred_element_type=jnp.float32
    )
    token_gradient = (
        frozen_output.reshape(segments_per_device, segment_token_rows, width_per_device)
        + ADAPTER_SCALE * adapter_output
    ) * live_rows[:, :, None]
    token_gradient = token_gradient.reshape(
        segments_per_device * segment_token_rows, width_per_device
    ).astype(jnp.bfloat16)
    gradient_scale = ADAPTER_SCALE / segment_token_rows
    segment_down_gradient = jnp.einsum(
        "upf,upb->ufb", gathered_weights, seg_tokens, preferred_element_type=jnp.float32
    )
    segment_up_gradient = jnp.einsum(
        "ija,ijn->ian", reduced_rows, seg_cotangent, preferred_element_type=jnp.float32
    )
    picker_f = owner_hit.astype(jnp.float32)
    slot_dgrad = (
        jnp.einsum("go,grd->ord", picker_f, segment_down_gradient, precision=lax.Precision.HIGHEST)
        * gradient_scale
    )
    slot_ugrad = (
        jnp.einsum("go,grk->ork", picker_f, segment_up_gradient, precision=lax.Precision.HIGHEST)
        * gradient_scale
    )
    slot_match = (wanted[:, None] == jnp.arange(places_per_device, dtype=jnp.int32)[None, :])[
        :, :, None, None
    ]
    dense_down = jnp.where(slot_match, slot_dgrad[:, None], 0.0).reshape(
        dp_count * places_per_device, rank_of_adapter, width_per_device
    )
    dense_up = jnp.where(slot_match, slot_ugrad[:, None], 0.0).reshape(
        dp_count * places_per_device, rank_of_adapter, key_dev
    )
    down_grad, up_grad = (
        lax.psum_scatter(dense_down, "dp", scatter_dimension=0, tiled=True),
        lax.psum_scatter(dense_up, "dp", scatter_dimension=0, tiled=True),
    )
    return (token_gradient, down_grad, up_grad)


def solution(mesh):
    placed = (
        P("dp", "tsp"),
        P("dp", "tsp"),
        P("tsp", None),
        P("dp", None, "tsp"),
        P("dp", None, "tsp"),
        P(),
        P("dp"),
        P("dp"),
    )
    return jax.shard_map(
        on_device,
        mesh=mesh,
        in_specs=placed,
        out_specs=(P("dp", "tsp"), P("dp", None, "tsp"), P("dp", None, "tsp")),
        check_vma=False,
    )
```

profile of v0, /device:TPU:2, one launch (start us, length us, event | category | flops | bytes accessed | tf_op | source)
XLA Modules:
  0.0 471.3 jit_solution(15498572598505192805)
XLA Ops:
  8.4 13.6 %all_to_all.19 = s32[32,1,1]{2,1,0:T(1,128)S(1)} all-to-all(s32[32,1,1]{2,1,0:T(1,128)S(1)} %copy.57), channel_id=1, replica_groups=mesh['dp'=32,'tsp'=8] {'dp'}, dimensions={0} | all-to-all | bytes 256 | tf_op jit(solution)/shard_map/all_to_all | solution.py:36
  22.6 1.1 convolution_convert_fusion.1
  24.8 5.0 %all-to-all-start.2 = ((bf16[32,64,128]{2,1,0:T(8,128)(2,1)}), bf16[32,64,128]{2,1,0:T(8,128)(2,1)S(1)}, u32[]{:S(2)}, u32[]{:S(2)}) async-start(bf16[32,64,128]{2,1,0:T(8,128)(2,1)} %copy.63), calls=%async_computation.2 | async-start | bytes 1048576 | tf_op jit(solution)/shard_map/all_to_all | solution.py:48
  29.8 2.3 convolution_convert_fusion
  32.0 4.3 copy.59
  36.4 3.9 all-to-all-done.2
  40.2 5.9 %all-to-all-start.1 = ((bf16[32,64,1024]{2,1,0:T(8,128)(2,1)}), bf16[32,64,1024]{2,1,0:T(8,128)(2,1)}, u32[]{:S(2)}, u32[]{:S(2)}) async-start(bf16[32,64,1024]{2,1,0:T(8,128)(2,1)} %copy.59), calls=%async_computation.1 | async-start | bytes 8388608 | tf_op jit(solution)/shard_map/all_to_all | solution.py:47
  47.3 50.4 %all-to-all-done.1 = bf16[32,64,1024]{2,1,0:T(8,128)(2,1)} async-done(((bf16[32,64,1024]{2,1,0:T(8,128)(2,1)}), bf16[32,64,1024]{2,1,0:T(8,128)(2,1)}, u32[]{:S(2)}, u32[]{:S(2)}) %all-to-all-start.1) | async-done | bytes 4194336 | tf_op jit(solution)/shard_map/all_to_all | solution.py:47
  97.7 6.9 %fusion.6 = bf16[16,64,1024]{2,0,1:T(8,128)(2,1)S(1)} fusion(bf16[32,64,1024]{2,1,0:T(8,128)(2,1)} %all-to-all-done.1, s32[16]{0:T(128)S(1)} %get-tuple-element.3), kind=kOutput, calls=%fused_computation.9 | convolution fusion | flops 68157952 | bytes 6291520 | tf_op jit(solution)/shard_map/go,ord->grd/dot_general | solution.py:51
  104.6 1.3 copy-done.1
  105.9 1.7 fusion.12
  107.6 1.1 pad_maximum_fusion
  109.8 75.4 %all-reduce.2.cloned.1.call-done = f32[16,128,128]{1,2,0:T(8,128)} async-done(((f32[16,128,128]{1,2,0:T(8,128)}), f32[16,128,128]{1,2,0:T(8,128)}) %all-reduce.2.cloned.1.call-update) | async-done | bytes 1048592 | tf_op jit(solution)/shard_map/psum | solution.py:73
  185.3 1.3 fusion.19
  188.1 1.5 bitcast_select_fusion.1
  189.9 2.9 fusion.24
  192.8 6.1 %broadcast_multiply_fusion = f32[32,64,1024]{2,0,1:T(8,128)S(1)} fusion(f32[16,64,1024]{2,1,0:T(8,128)S(1)} %fusion.24, s32[16]{0:T(128)S(1)} %get-tuple-element.3), kind=kOutput, calls=%fused_computation.6 | convolution fusion | flops 404750848 | bytes 12582976 | tf_op jit(solution)/shard_map/go,grd->ord/dot_general | solution.py:101
  198.9 8.1 %copy.68 = f32[32,64,1024]{2,1,0:T(8,128)} copy(f32[32,64,1024]{2,0,1:T(8,128)S(1)} %broadcast_multiply_fusion) | data formatting | bytes 16777216 | tf_op jit(solution)/shard_map/mul | solution.py:101
  207.0 12.7 %bitcast_select_fusion = f32[64,64,1024]{2,1,0:T(8,128)} fusion(f32[32,64,1024]{2,1,0:T(8,128)} %copy.68, pred[64]{0:T(512)(128)(4,1)S(1)} %eq.76), kind=kLoop, calls=%fused_computation | loop fusion | flops 4194304 | bytes 25165888 | tf_op jit(solution)/shard_map/jit(_where)/select_n | solution.py:111
  219.8 28.1 %all-gather.2.cloned.1.call-done = bf16[2048,1024]{1,0:T(8,128)(2,1)} async-done(((bf16[2048,128]{1,0:T(8,128)(2,1)}), bf16[2048,1024]{1,0:T(8,128)(2,1)}) %all-gather.2.cloned.1.call-update) | async-done | bytes 4194320 | tf_op jit(solution)/shard_map/all_gather | solution.py:77
  247.9 6.5 %fusion.42 = f32[2048,1024]{1,0:T(8,128)S(1)} fusion(bf16[2048,1024]{1,0:T(8,128)(2,1)} %all-gather.2.cloned.1.call-done, bf16[1024,1024]{1,0:T(8,128)(2,1)S(1)} %copy-done), kind=kOutput, calls=%fused_computation.53 | convolution fusion | flops 4294967296 | bytes 14680064 | tf_op jit(solution)/shard_map/dot_general | solution.py:76
  254.4 5.2 %multiply_convert_fusion = bf16[16,128,1024]{2,1,0:T(8,128)(2,1)} fusion(f32[16,128,1024]{2,1,0:T(8,128)S(1)} %bitcast.32, f32[16,128]{1,0:T(8,128)S(1)} %fusion.33, bf16[16,64,1024]{2,0,1:T(8,128)(2,1)S(1)} %copy-done.2, f32[16,128,128]{1,2,0:T(8,128)S(1)} %copy-done.6), kind=kOutput, calls=%fused_computation.1 | convolution fusion | flops 277086208 | bytes 15220736 | tf_op jit(solution)/shard_map/wks,wsx->wkx/dot_general | solution.py:82
  259.7 77.8 %reduce-scatter.5.cloned.1.call-done = f32[2,64,128]{2,1,0:T(8,128)} async-done(((f32[64,64,128]{2,1,0:T(8,128)}), f32[2,64,128]{2,1,0:T(8,128)}) %reduce-scatter.5.cloned.1.call-update) | async-done | bytes 65552 | tf_op jit(solution)/shard_map/reduce_scatter | solution.py:119
  337.5 127.2 %reduce-scatter.3.cloned.1.call-done = f32[2,64,1024]{2,1,0:T(8,128)} async-done(((f32[64,64,1024]{2,1,0:T(8,128)}), f32[2,64,1024]{2,1,0:T(8,128)}) %reduce-scatter.3.cloned.1.call-update) | async-done | bytes 524304 | tf_op jit(solution)/shard_map/reduce_scatter | solution.py:118
  (36 shorter events, 6.8 us)
Async XLA Ops:
  7.2 240.8 %copy-start = (bf16[1024,1024]{1,0:T(8,128)(2,1)S(1)}, bf16[1024,1024]{1,0:T(8,128)(2,1)}, u32[]{:S(2)}) copy-start(bf16[1024,1024]{1,0:T(8,128)(2,1)} %param.10) | copy-start | bytes 6291460
  24.8 15.5 %all-to-all-start.2 = ((bf16[32,64,128]{2,1,0:T(8,128)(2,1)}), bf16[32,64,128]{2,1,0:T(8,128)(2,1)S(1)}, u32[]{:S(2)}, u32[]{:S(2)}) async-start(bf16[32,64,128]{2,1,0:T(8,128)(2,1)} %copy.63), calls=%async_computation.2 | async-start | bytes 1048576 | tf_op jit(solution)/shard_map/all_to_all | solution.py:48
  36.4 10.4 %copy-start.4 = (bf16[2048,128]{1,0:T(8,128)(2,1)S(1)}, bf16[2048,128]{1,0:T(8,128)(2,1)}, u32[]{:S(2)}) copy-start(bf16[2048,128]{1,0:T(8,128)(2,1)} %param.9) | copy-start | bytes 1572868
  40.2 57.4 %all-to-all-start.1 = ((bf16[32,64,1024]{2,1,0:T(8,128)(2,1)}), bf16[32,64,1024]{2,1,0:T(8,128)(2,1)}, u32[]{:S(2)}, u32[]{:S(2)}) async-start(bf16[32,64,1024]{2,1,0:T(8,128)(2,1)} %copy.59), calls=%async_computation.1 | async-start | bytes 8388608 | tf_op jit(solution)/shard_map/all_to_all | solution.py:47
  46.2 139.1 %all-reduce.2.cloned.1.call-start = ((), (), s32[]{:S(2)}) async-start(), calls=%async_computation.6 | async-start | bytes 2097152 | tf_op jit(solution)/shard_map/psum | solution.py:73
  97.7 8.2 %copy-start.3 = (bf16[2048,1024]{1,0:T(8,128)(2,1)S(1)}, bf16[2048,1024]{1,0:T(8,128)(2,1)}, u32[]{:S(2)}) copy-start(bf16[2048,1024]{1,0:T(8,128)(2,1)} %param.8) | copy-start | bytes 12582916
  104.6 1.3 copy-start.1
  105.9 3.9 copy-start.7
  105.9 79.4 %copy-start.5 = (bf16[2048,128]{1,0:T(8,128)(2,1)S(1)}, bf16[2048,128]{1,0:T(8,128)(2,1)}, u32[]{:S(2)}) copy-start(bf16[2048,128]{1,0:T(8,128)(2,1)} %param.9) | copy-start | bytes 1572868
  108.8 139.1 %all-gather.2.cloned.1.call-start = ((), (), s32[]{:S(2)}) async-start(), calls=%async_computation.5 | async-start | bytes 4718592 | tf_op jit(solution)/shard_map/all_gather | solution.py:77
  109.5 228.0 %reduce-scatter.5.cloned.1.call-start = ((), (), s32[]{:S(2)}) async-start(), calls=%async_computation.8 | async-start | bytes 2162688 | tf_op jit(solution)/shard_map/reduce_scatter | solution.py:119
  186.6 3.4 copy-start.6
  189.7 275.1 %reduce-scatter.3.cloned.1.call-start = ((), (), s32[]{:S(2)}) async-start(), calls=%async_computation.7 | async-start | bytes 17301504 | tf_op jit(solution)/shard_map/reduce_scatter | solution.py:118
  247.9 6.5 %copy-start.2 = (bf16[16,64,1024]{2,0,1:T(8,128)(2,1)S(1)}, bf16[16,64,1024]{2,0,1:T(8,128)(2,1)}, u32[]{:S(2)}) copy-start(bf16[16,64,1024]{2,0,1:T(8,128)(2,1)} %copy-done.1) | copy-start | bytes 6291460
Sparse Core Ops, SparseCore 0:
  108.9 76.3 all-reduce.1
  187.0 60.8 all-gather.1
  252.3 85.1 reduce-scatter.4
  342.1 122.5 reduce-scatter.2
where the time goes:
time: 472 us; the launch traced here: 471 us
  waiting for transfers between devices  364 us (77%)
  matrix products  35.8 us (8%)
  other arithmetic  17.3 us (4%)
  local copies, waits for them, and re-layouts  15.6 us (3%)
  between operations  13.9 us (3%)
  blocking collectives  13.6 us (3%)
  starting transfers between devices  11.5 us (2%)
    reduce_scatter x1, waiting for transfers between devices, on_device(): lax.psum_scatter(dense_down, 'dp', scatter_dimension=0, tiled=True)  127 us
    reduce_scatter x1, waiting for transfers between devices, on_device(): lax.psum_scatter(dense_up, 'dp', scatter_dimension=0, tiled=True)  77.8 us
    psum x1, waiting for transfers between devices, on_device(): summed = lax.psum(partial_terms, 'tsp')  75.4 us
    all_to_all x1, waiting for transfers between devices, on_device(): lax.all_to_all(reply_down, 'dp', split_axis=0, concat_axis=0, tiled=True)  50.4 us
    all_gather x1, waiting for transfers between devices, on_device(): lax.all_gather(cotangent, 'tsp', axis=1, tiled=True)  28.1 us
    all_to_all x1, blocking collectives, on_device(): lax.all_to_all(wanted[:, None], 'dp', split_axis=0, concat_axis=0, tiled=...  13.6 us
    select_n x1, other arithmetic, on_device(): jnp.where(slot_match, slot_dgrad[:, None], 0.0)  12.7 us
  transfers between devices with their start and end apart: 6, of which 6 were waited for; matrix products, arithmetic and copies ran while one was open for 11% of the time, Pallas kernels for 0%

commit v1 on v0

--- a/solution.py
+++ b/solution.py
@@ -74,7 +74,9 @@
     reduced_rows = (summed[:, :, :rank_of_adapter] * live_rows[:, :, None]).astype(jnp.bfloat16)
     gathered_weights = (summed[:, :, rank_of_adapter:] * live_rows[:, :, None]).astype(jnp.bfloat16)
     frozen_output = lax.dot_general(
-        lax.all_gather(cotangent, "tsp", axis=1, tiled=True),
+        jnp.concatenate(
+            lax.all_to_all(jnp.stack([cotangent] * lax.axis_size("tsp")), "tsp", 0, 0), axis=1
+        ),
         frozen_key_weight,
         (((1,), (1,)), ((), ())),
         preferred_element_type=jnp.float32,

time: 472 us -> 414 us (0.88)
  waiting for transfers between devices: 364 us -> 184 us
  blocking collectives: 13.6 us -> 109 us
  local copies, waits for them, and re-layouts: 15.6 us -> 36.6 us
    all_to_all x0 -> x1, blocking collectives: none -> 95.7 us  [on_device(): lax.all_to_all(jnp.stack([cotangent] * lax.axis_size('tsp')), 'tsp', 0, 0)]
    reduce_scatter x1, waiting for transfers between devices: 77.8 us -> 0.01 us  [on_device(): lax.psum_scatter(dense_up, 'dp', scatter_dimension=0, tiled=True)]
    reduce_scatter x1, waiting for transfers between devices: 127 us -> 53.3 us  [on_device(): lax.psum_scatter(dense_down, 'dp', scatter_dimension=0, tiled=True)]
    all_gather x1 -> x0, waiting for transfers between devices: 28.1 us -> none  [on_device(): lax.all_gather(cotangent, 'tsp', axis=1, tiled=True)]
    reshape x0 -> x1, local copies, waits for them, and re-layouts: none -> 13.2 us  [on_device(): jnp.concatenate(lax.all_to_all(jnp.stack([cotangent] * lax.axis_size('tsp...]
    dot_general x0 -> x1, local copies, waits for them, and re-layouts: none -> 7.28 us  [on_device(): lax.dot_general(jnp.concatenate(lax.all_to_all(jnp.stack([cotangent] * la...]
  transfers between devices with their start and end apart: 6 -> 5, of which waited for: 6 -> 4; matrix products, arithmetic and copies ran while one was open for 11% -> 17% of each run, Pallas kernels for 0% -> 0%
where the time goes in v1:
time: 414 us; the launch traced here: 409 us
  waiting for transfers between devices  184 us (44%)
  blocking collectives  109 us (26%)
  local copies, waits for them, and re-layouts  36.6 us (9%)
  matrix products  36.2 us (9%)
  other arithmetic  17.3 us (4%)
  between operations  14.1 us (3%)
  starting transfers between devices  11.6 us (3%)
    all_to_all x1, blocking collectives, on_device(): lax.all_to_all(jnp.stack([cotangent] * lax.axis_size('tsp')), 'tsp', 0, 0)  95.7 us
    psum x1, waiting for transfers between devices, on_device(): summed = lax.psum(partial_terms, 'tsp')  76.2 us
    reduce_scatter x1, waiting for transfers between devices, on_device(): lax.psum_scatter(dense_down, 'dp', scatter_dimension=0, tiled=True)  53.3 us
    all_to_all x1, waiting for transfers between devices, on_device(): lax.all_to_all(reply_down, 'dp', split_axis=0, concat_axis=0, tiled=True)  50.1 us
    all_to_all x1, blocking collectives, on_device(): lax.all_to_all(wanted[:, None], 'dp', split_axis=0, concat_axis=0, tiled=...  13.6 us
    reshape x1, local copies, waits for them, and re-layouts, on_device(): jnp.concatenate(lax.all_to_all(jnp.stack([cotangent] * lax.axis_size('tsp...  13.2 us
    select_n x1, other arithmetic, on_device(): jnp.where(slot_match, slot_dgrad[:, None], 0.0)  12.8 us
  transfers between devices with their start and end apart: 5, of which 4 were waited for; matrix products, arithmetic and copies ran while one was open for 17% of the time, Pallas kernels for 0%

profile of v1, /device:TPU:2, one launch (start us, length us, event | category | flops | bytes accessed | tf_op | source)
XLA Modules:
  0.0 408.7 jit_solution(14124886071564476128)
XLA Ops:
  8.4 13.6 %all_to_all.24 = s32[32,1,1]{2,1,0:T(1,128)S(1)} all-to-all(s32[32,1,1]{2,1,0:T(1,128)S(1)} %copy.61), channel_id=1, replica_groups=mesh['dp'=32,'tsp'=8] {'dp'}, dimensions={0} | all-to-all | bytes 256 | tf_op jit(solution)/shard_map/all_to_all | solution.py:36
  22.6 1.1 convolution_convert_fusion.1
  24.8 5.0 %all-to-all-start.3 = ((bf16[32,64,128]{2,1,0:T(8,128)(2,1)}), bf16[32,64,128]{2,1,0:T(8,128)(2,1)S(1)}, u32[]{:S(2)}, u32[]{:S(2)}) async-start(bf16[32,64,128]{2,1,0:T(8,128)(2,1)} %copy.67), calls=%async_computation.3 | async-start | bytes 1048576 | tf_op jit(solution)/shard_map/all_to_all | solution.py:48
  29.8 2.3 convolution_convert_fusion
  32.0 4.3 %copy.63 = bf16[32,64,1024]{2,1,0:T(8,128)(2,1)} copy(bf16[32,64,1024]{2,0,1:T(8,128)(2,1)S(1)} %convolution_convert_fusion) | data formatting | bytes 8388608 | tf_op jit(solution)/shard_map/convert_element_type | solution.py:42
  36.4 3.9 all-to-all-done.3
  40.2 5.9 %all-to-all-start.2 = ((bf16[32,64,1024]{2,1,0:T(8,128)(2,1)}), bf16[32,64,1024]{2,1,0:T(8,128)(2,1)}, u32[]{:S(2)}, u32[]{:S(2)}) async-start(bf16[32,64,1024]{2,1,0:T(8,128)(2,1)} %copy.63), calls=%async_computation.2 | async-start | bytes 8388608 | tf_op jit(solution)/shard_map/all_to_all | solution.py:47
  47.5 50.1 %all-to-all-done.2 = bf16[32,64,1024]{2,1,0:T(8,128)(2,1)} async-done(((bf16[32,64,1024]{2,1,0:T(8,128)(2,1)}), bf16[32,64,1024]{2,1,0:T(8,128)(2,1)}, u32[]{:S(2)}, u32[]{:S(2)}) %all-to-all-start.2) | async-done | bytes 4194336 | tf_op jit(solution)/shard_map/all_to_all | solution.py:47
  97.7 6.9 %fusion.8 = bf16[16,64,1024]{2,0,1:T(8,128)(2,1)S(1)} fusion(bf16[32,64,1024]{2,1,0:T(8,128)(2,1)} %all-to-all-done.2, s32[16]{0:T(128)S(1)} %get-tuple-element.3), kind=kOutput, calls=%fused_computation.11 | convolution fusion | flops 68157952 | bytes 6291520 | tf_op jit(solution)/shard_map/go,ord->grd/dot_general | solution.py:51
  104.6 1.4 copy-done.1
  105.9 1.7 fusion.14
  109.1 76.2 %all-reduce.2.cloned.1.call-done = f32[16,128,128]{1,2,0:T(8,128)} async-done(((f32[16,128,128]{1,2,0:T(8,128)}), f32[16,128,128]{1,2,0:T(8,128)}) %all-reduce.2.cloned.1.call-update) | async-done | bytes 1048592 | tf_op jit(solution)/shard_map/psum | solution.py:73
  185.3 1.3 fusion.21
  188.1 1.5 bitcast_select_fusion.1
  189.9 3.1 fusion.26
  192.9 6.1 %broadcast_multiply_fusion = f32[32,64,1024]{2,0,1:T(8,128)S(1)} fusion(f32[16,64,1024]{2,1,0:T(8,128)S(1)} %fusion.26, s32[16]{0:T(128)S(1)} %get-tuple-element.3), kind=kOutput, calls=%fused_computation.6 | convolution fusion | flops 404750848 | bytes 12582976 | tf_op jit(solution)/shard_map/go,grd->ord/dot_general | solution.py:103
  199.0 8.1 %copy.72 = f32[32,64,1024]{2,1,0:T(8,128)} copy(f32[32,64,1024]{2,0,1:T(8,128)S(1)} %broadcast_multiply_fusion) | data formatting | bytes 16777216 | tf_op jit(solution)/shard_map/mul | solution.py:103
  207.1 12.8 %bitcast_select_fusion = f32[64,64,1024]{2,1,0:T(8,128)} fusion(f32[32,64,1024]{2,1,0:T(8,128)} %copy.72, pred[64]{0:T(512)(128)(4,1)S(1)} %eq.76), kind=kLoop, calls=%fused_computation | loop fusion | flops 4194304 | bytes 25165888 | tf_op jit(solution)/shard_map/jit(_where)/select_n | solution.py:113
  220.5 95.7 %all_to_all.25 = bf16[8,2048,128]{2,1,0:T(8,128)(2,1)S(1)} all-to-all(bf16[8,2048,128]{2,1,0:T(8,128)(2,1)S(1)} %stack.2), channel_id=1, replica_groups=mesh['dp'=32,'tsp'=8] {'tsp'}, dimensions={0} | all-to-all | bytes 8388608 | tf_op jit(solution)/shard_map/all_to_all | solution.py:78
  316.1 13.2 %copy.60 = bf16[2048,8,128]{2,1,0:T(8,128)(2,1)} copy(bf16[2048,8,128]{2,0,1:T(8,128)(2,1)S(1)} %bitcast.34) | data formatting | bytes 8388608 | tf_op jit(solution)/shard_map/reshape | solution.py:77
  329.3 7.3 %dot_general.42 = bf16[16,128,1024]{2,1,0:T(8,128)(2,1)} reshape(bf16[2048,8,128]{2,1,0:T(8,128)(2,1)} %copy.60) | data formatting | bytes 8388608 | tf_op jit(solution)/shard_map/dot_general | solution.py:76
  336.6 6.8 %fusion.6 = f32[16,128,1024]{2,1,0:T(8,128)S(1)} fusion(bf16[16,128,1024]{2,1,0:T(8,128)(2,1)} %dot_general.42, bf16[1024,1024]{1,0:T(8,128)(2,1)S(1)} %copy-done), kind=kOutput, calls=%fused_computation.9 | convolution fusion | flops 4294967296 | bytes 14680064 | tf_op jit(solution)/shard_map/dot_general | solution.py:76
  343.4 5.2 %multiply_convert_fusion = bf16[16,128,1024]{2,1,0:T(8,128)(2,1)} fusion(f32[16,128,1024]{2,1,0:T(8,128)S(1)} %fusion.6, f32[16,128]{1,0:T(8,128)S(1)} %fusion.35, bf16[16,64,1024]{2,0,1:T(8,128)(2,1)S(1)} %copy-done.2, f32[16,128,128]{1,2,0:T(8,128)S(1)} %copy-done.5), kind=kOutput, calls=%fused_computation.1 | convolution fusion | flops 277086208 | bytes 15220736 | tf_op jit(solution)/shard_map/wks,wsx->wkx/dot_general | solution.py:84
  348.6 53.3 %reduce-scatter.3.cloned.1.call-done = f32[2,64,1024]{2,1,0:T(8,128)} async-done(((f32[64,64,1024]{2,1,0:T(8,128)}), f32[2,64,1024]{2,1,0:T(8,128)}) %reduce-scatter.3.cloned.1.call-update) | async-done | bytes 524304 | tf_op jit(solution)/shard_map/reduce_scatter | solution.py:120
  (35 shorter events, 7.9 us)
Async XLA Ops:
  7.2 329.4 %copy-start = (bf16[1024,1024]{1,0:T(8,128)(2,1)S(1)}, bf16[1024,1024]{1,0:T(8,128)(2,1)}, u32[]{:S(2)}) copy-start(bf16[1024,1024]{1,0:T(8,128)(2,1)} %param.10) | copy-start | bytes 6291460
  24.8 15.5 %all-to-all-start.3 = ((bf16[32,64,128]{2,1,0:T(8,128)(2,1)}), bf16[32,64,128]{2,1,0:T(8,128)(2,1)S(1)}, u32[]{:S(2)}, u32[]{:S(2)}) async-start(bf16[32,64,128]{2,1,0:T(8,128)(2,1)} %copy.67), calls=%async_computation.3 | async-start | bytes 1048576 | tf_op jit(solution)/shard_map/all_to_all | solution.py:48
  36.4 10.7 %copy-start.4 = (bf16[2048,128]{1,0:T(8,128)(2,1)S(1)}, bf16[2048,128]{1,0:T(8,128)(2,1)}, u32[]{:S(2)}) copy-start(bf16[2048,128]{1,0:T(8,128)(2,1)} %param.9) | copy-start | bytes 1572868
  40.2 57.4 %all-to-all-start.2 = ((bf16[32,64,1024]{2,1,0:T(8,128)(2,1)}), bf16[32,64,1024]{2,1,0:T(8,128)(2,1)}, u32[]{:S(2)}, u32[]{:S(2)}) async-start(bf16[32,64,1024]{2,1,0:T(8,128)(2,1)} %copy.63), calls=%async_computation.2 | async-start | bytes 8388608 | tf_op jit(solution)/shard_map/all_to_all | solution.py:47
  46.1 139.1 %all-reduce.2.cloned.1.call-start = ((), (), s32[]{:S(2)}) async-start(), calls=%async_computation.6 | async-start | bytes 2097152 | tf_op jit(solution)/shard_map/psum | solution.py:73
  97.7 8.3 %copy-start.3 = (bf16[2048,1024]{1,0:T(8,128)(2,1)S(1)}, bf16[2048,1024]{1,0:T(8,128)(2,1)}, u32[]{:S(2)}) copy-start(bf16[2048,1024]{1,0:T(8,128)(2,1)} %param.8) | copy-start | bytes 12582916
  104.6 1.4 copy-start.1
  105.9 3.1 copy-start.6
  108.7 239.9 %reduce-scatter.5.cloned.1.call-start = ((), (), s32[]{:S(2)}) async-start(), calls=%async_computation.8 | async-start | bytes 2162688 | tf_op jit(solution)/shard_map/reduce_scatter | solution.py:121
  189.6 212.3 %reduce-scatter.3.cloned.1.call-start = ((), (), s32[]{:S(2)}) async-start(), calls=%async_computation.7 | async-start | bytes 17301504 | tf_op jit(solution)/shard_map/reduce_scatter | solution.py:120
  336.6 6.8 %copy-start.2 = (bf16[16,64,1024]{2,0,1:T(8,128)(2,1)S(1)}, bf16[16,64,1024]{2,0,1:T(8,128)(2,1)}, u32[]{:S(2)}) copy-start(bf16[16,64,1024]{2,0,1:T(8,128)(2,1)} %copy-done.1) | copy-start | bytes 6291460
  336.6 6.8 %copy-start.5 = (f32[16,128,128]{1,2,0:T(8,128)S(1)}, f32[16,128,128]{1,2,0:T(8,128)}, u32[]{:S(2)}) copy-start(f32[16,128,128]{1,2,0:T(8,128)} %all-reduce.2.cloned.1.call-done) | copy-start | bytes 3145732
Sparse Core Ops, SparseCore 0:
  108.9 76.3 all-reduce.1
  189.8 84.7 reduce-scatter.4
  279.4 122.5 reduce-scatter.2
